TPU v7x, 768 devices: a whole 4x8x12 slice. The times are simulated.
768 devices in a mesh: freq: 96 (over z, x, y_hi), depth: 8 (over y_lo, core).
Axes of the slice: x: 4, y: 8 (y_hi: 2, y_lo: 4; y = y_hi * 4 + y_lo), z: 12, core: 2. Of those that a mesh axis runs over, the one named last changes fastest.
Arguments:
- slowness: float32 [8, 24576], P('depth', 'freq'), may hold values from 0.25 to 1
- freq_index: int32 [192], P('freq'), may hold values from 0 to 191, each once
- taps: float32 [192, 2, 11], replicated, may hold values from -1 to 1, as said below
- source_top: float32 [192, 8, 2, 24, 1024], P('freq', 'depth'), may hold values from -6 to 6
- adjoint_source: float32 [192, 8, 2, 24, 1024], P('freq', 'depth'), may hold values from -6 to 6
Outputs:
- gradient: float32 [8, 24576], P('depth', 'freq')
Inputs may be any that keep to these rules, and one draw needn't show every extreme that they name: `freq_index`: each of 0 to 191 appears once. In each frequency the absolute values of the complex taps sum to at most 1.
All inputs are finite; a program needn't handle non-finite values.
Results may differ from a plain program's by a relative error of at most 0.0003.
Values sent between devices are 32-bit elements; how exact they have to be, the bound alone decides.
No kernel may reach another device: no remote copies, remote signals or barrier semaphores. Data moves between devices by JAX's collectives and lax.ppermute only.
A program may use at most 32 MiB of HBM per device.

v0:
```python
import jax
import jax.numpy as jnp
from jax import lax
from jax.sharding import PartitionSpec as P


def from_behind(value, axis, steps):
    count = lax.axis_size(axis)
    leading, last = (max(0, -steps), min(count, count - steps))
    return lax.ppermute(value, axis, [(source, source + steps) for source in range(leading, last)])


def convolve(field_re, field_im, tap_re, tap_im, along, adjoint):
    along = field_re.ndim + along
    reach = tap_re.shape[-1] // 2
    extent = field_re.shape[along]
    widths = [(0, 0)] * field_re.ndim
    widths[along] = (reach, reach)
    padded_re = jnp.pad(field_re, widths)
    padded_im = jnp.pad(field_im, widths)
    out_re = jnp.zeros_like(field_re)
    out_im = jnp.zeros_like(field_im)
    for offset in range(2 * reach + 1):
        anchor = 2 * reach - offset if adjoint else offset
        shifted_re = lax.slice_in_dim(padded_re, anchor, anchor + extent, axis=along)
        shifted_im = lax.slice_in_dim(padded_im, anchor, anchor + extent, axis=along)
        coef_re = tap_re[..., offset][..., None, None]
        coef_im = tap_im[..., offset][..., None, None]
        if adjoint:
            out_re = out_re + coef_re * shifted_re + coef_im * shifted_im
            out_im = out_im + coef_re * shifted_im - coef_im * shifted_re
        else:
            out_re = out_re + coef_re * shifted_re - coef_im * shifted_im
            out_im = out_im + coef_re * shifted_im + coef_im * shifted_re
    return (out_re, out_im)


def forward_step(field_re, field_im, tap_re, tap_im, phase_cos, phase_sin):
    mid_re, mid_im = convolve(field_re, field_im, tap_re, tap_im, -1, False)
    mid_re, mid_im = convolve(mid_re, mid_im, tap_re, tap_im, -2, False)
    return (phase_cos * mid_re - phase_sin * mid_im, phase_sin * mid_re + phase_cos * mid_im)


def adjoint_step(field_re, field_im, tap_re, tap_im, phase_cos, phase_sin):
    mid_re = phase_cos * field_re + phase_sin * field_im
    mid_im = phase_cos * field_im - phase_sin * field_re
    mid_re, mid_im = convolve(mid_re, mid_im, tap_re, tap_im, -2, True)
    return convolve(mid_re, mid_im, tap_re, tap_im, -1, True)


def sweep(
    incoming, adj_re, adj_im, wave_re, wave_im, phase_cos, phase_sin, tap_re, tap_im, angular
):
    steps = adj_re.shape[1]
    carry = (incoming[:, 0], incoming[:, 1])
    terms = [None] * steps
    for step in reversed(range(steps)):
        mu_re = adj_re[:, step] + carry[0]
        mu_im = adj_im[:, step] + carry[1]
        terms[step] = jnp.sum(
            angular[:, None, None] * (mu_im * wave_re[:, step] - mu_re * wave_im[:, step]), axis=0
        )
        carry = adjoint_step(mu_re, mu_im, tap_re, tap_im, phase_cos[:, step], phase_sin[:, step])
    return (jnp.stack(carry, axis=1), jnp.stack(terms))


def on_device(slowness, freq_index, taps, source_top, adjoint_source):
    steps = slowness.shape[0]
    lines, cells = (source_top.shape[3], source_top.shape[4])
    whole = lax.all_gather(slowness, "freq", axis=1, tiled=True).reshape(steps, lines, cells)
    count = taps.shape[0]
    lanes = freq_index.shape[0]
    onehot = (freq_index[:, None] == jnp.arange(count, dtype=jnp.int32)[None, :]).astype(
        jnp.float32
    )
    tap_table = jnp.dot(
        onehot,
        taps.reshape(count, -1),
        precision=lax.Precision.HIGHEST,
        preferred_element_type=jnp.float32,
    ).reshape(lanes, 2, -1)
    tap_re, tap_im = (tap_table[:, 0], tap_table[:, 1])
    angular = 8.0 * (freq_index.astype(jnp.float32) + 1.0) / count
    phase = angular[:, None, None, None] * whole[None]
    phase_cos = jnp.cos(phase)
    phase_sin = jnp.sin(phase)
    field_re, field_im = (source_top[:, 0, 0], source_top[:, 0, 1])
    waves_re, waves_im = ([], [])
    field_re, field_im = forward_step(
        field_re, field_im, tap_re, tap_im, phase_cos[:, 0], phase_sin[:, 0]
    )
    waves_re.append(field_re)
    waves_im.append(field_im)
    wave_re = jnp.stack(waves_re, axis=1)
    wave_im = jnp.stack(waves_im, axis=1)
    adj_re = adjoint_source[:, :, 0]
    adj_im = adjoint_source[:, :, 1]
    depth_count = lax.axis_size("depth")

    def segment(turn, received):
        top, _ = sweep(
            received,
            adj_re,
            adj_im,
            wave_re,
            wave_im,
            phase_cos,
            phase_sin,
            tap_re,
            tap_im,
            angular,
        )
        return from_behind(top, "depth", -1)

    received = lax.fori_loop(
        0, depth_count - 1, segment, jnp.zeros((lanes, 2, lines, cells), jnp.float32)
    )
    _, image = sweep(
        received, adj_re, adj_im, wave_re, wave_im, phase_cos, phase_sin, tap_re, tap_im, angular
    )
    summed = lax.psum_scatter(
        image.reshape(steps, lines * cells), "freq", scatter_dimension=1, tiled=True
    )
    return summed / count


def solution(mesh):
    in_specs = (
        P("depth", "freq"),
        P("freq"),
        P(),
        P("freq", "depth", None, None, None),
        P("freq", "depth", None, None, None),
    )
    out_specs = P("depth", "freq")
    return jax.shard_map(
        on_device, mesh=mesh, in_specs=in_specs, out_specs=out_specs, check_vma=False
    )
```

profile of v0, /device:TPU:24, one launch (start us, length us, event | category | flops | bytes accessed | tf_op | source)
XLA Modules:
  0.0 1166.1 jit_solution(9328358154999074256)
XLA Ops:
  6.5 0.7 add_multiply_fusion
  7.2 0.7 copy.20
  7.9 0.8 fusion.23
  9.7 1.1 slice_bitcast_fusion.23
  10.7 1.1 multiply_subtract_fusion.1
  11.9 1.1 multiply_add_fusion.1
  13.0 336.1 %all_gather.3 = f32[1,24576]{1,0:T(1,128)S(1)} all-gather(f32[1,256]{1,0:T(1,128)} %param.7), channel_id=1, replica_groups=mesh['freq'=96,'depth'=8] {'freq'}, dimensions={1}, use_global_device_ids=true | all-gather | bytes 99328 | tf_op jit(solution)/shard_map/all_gather | solution.py:70
  349.7 0.9 reduce.47
  350.7 1.1 slice_bitcast_fusion.25
  351.8 92.9 %while.14 = (s32[]{:T(128)}, f32[2,2,24,1024]{3,2,0,1:T(8,128)S(1)}, f32[2,11]{0,1:T(8,128)S(1)}, f32[2,1,1,24,1024]{4,3,0,2,1:T(8,128)S(1)}, f32[2,1,1,24,1024]...) while((s32[]{:T(128)}, ...), condition=%wide.region_1.2_spmd.clone.clone, body=%wide.region_0.1_spmd.clone.clone.sunk | while | flops 8994818 | bytes 5997741 | solution.py:115
  351.8 0.8 fusion.30
  352.6 0.6 multiply_subtract_fusion.3
  353.3 0.6 multiply_add_fusion.3
  353.9 1.1 add_bitcast_fusion.2
  355.1 1.1 subtract_bitcast_fusion.2
  356.2 1.9 collective-permute-start
  358.2 5.3 collective-permute-done
  363.5 0.8 fusion.30
  364.3 0.6 multiply_subtract_fusion.3
  364.9 0.6 multiply_add_fusion.3
  365.6 1.1 add_bitcast_fusion.2
  366.7 1.1 subtract_bitcast_fusion.2
  367.9 3.8 collective-permute-start
  371.7 5.3 collective-permute-done
  377.0 0.8 fusion.30
  377.8 0.6 multiply_subtract_fusion.3
  378.4 0.6 multiply_add_fusion.3
  379.1 1.1 add_bitcast_fusion.2
  380.2 1.1 subtract_bitcast_fusion.2
  381.4 3.8 collective-permute-start
  385.2 5.3 collective-permute-done
  390.5 0.8 fusion.30
  391.3 0.6 multiply_subtract_fusion.3
  392.0 0.6 multiply_add_fusion.3
  392.6 1.1 add_bitcast_fusion.2
  393.8 1.1 subtract_bitcast_fusion.2
  394.9 3.8 collective-permute-start
  398.8 5.3 collective-permute-done
  404.0 0.8 fusion.30
  404.9 0.6 multiply_subtract_fusion.3
  405.5 0.6 multiply_add_fusion.3
  406.2 1.1 add_bitcast_fusion.2
  407.3 1.1 subtract_bitcast_fusion.2
  408.5 3.8 collective-permute-start
  412.3 5.3 collective-permute-done
  417.6 0.8 fusion.30
  418.4 0.6 multiply_subtract_fusion.3
  419.0 0.6 multiply_add_fusion.3
  419.7 1.1 add_bitcast_fusion.2
  420.8 1.1 subtract_bitcast_fusion.2
  422.0 3.8 collective-permute-start
  425.8 5.3 collective-permute-done
  431.1 0.8 fusion.30
  431.9 0.6 multiply_subtract_fusion.3
  432.6 0.6 multiply_add_fusion.3
  433.2 1.1 add_bitcast_fusion.2
  434.4 1.1 subtract_bitcast_fusion.2
  435.5 3.8 collective-permute-start
  439.4 5.3 collective-permute-done
  444.6 1.9 fusion.20
  446.6 6.8 copy.33
  453.4 10.0 bitcast_bitcast_fusion
  463.4 694.3 %reduce-scatter.4.cloned.1.call-done = f32[256,1]{1,0:T(8,128)} async-done(((f32[24576,1]{1,0:T(8,128)}), f32[256,1]{1,0:T(8,128)}) %reduce-scatter.4.cloned.1.call-update) | async-done | bytes 1040
  1157.7 1.0 copy.27
  (37 shorter events, 2.6 us)
Async XLA Ops:
  6.5 1151.2 %reduce-scatter.4.cloned.1.call-start = ((), (), s32[]{:S(2)}) async-start(), calls=%async_computation.1 | async-start | bytes 12713984
  11.9 432.8 %copy-start = (f32[2,1,2,24,1024]{4,3,2,1,0:T(8,128)S(1)}, f32[2,1,2,24,1024]{4,3,2,1,0:T(8,128)}, u32[]{:S(2)}) copy-start(f32[2,1,2,24,1024]{4,3,2,1,0:T(8,128)} %param.11) | copy-start | bytes 1179652
  356.2 7.2 collective-permute-start
  367.9 9.1 collective-permute-start
  381.4 9.1 collective-permute-start
  394.9 9.1 collective-permute-start
  408.5 9.1 collective-permute-start
  422.0 9.1 collective-permute-start
  435.5 9.1 collective-permute-start
Sparse Core Ops, SparseCore 0:
  463.5 694.1 reduce-scatter.3
where the time goes:
time: 1170 us
  waiting for transfers between devices  731 us (62%)
  blocking collectives  336 us (29%)
  other arithmetic  37 us (3%)
  starting transfers between devices  24.8 us (2%)
  local copies, waits for them, and re-layouts  22.4 us (2%)
  between operations  13.5 us (1%)
    unnamed x2, waiting for transfers between devices  694 us
    all_gather x1, blocking collectives, on_device(): lax.all_gather(slowness, 'freq', axis=1, tiled=True)  336 us
    ppermute x7, waiting for transfers between devices, from_behind(): lax.ppermute(value, axis, [(source, source + steps) for source in range(l...  36.9 us
    ppermute x7, starting transfers between devices, from_behind(): lax.ppermute(value, axis, [(source, source + steps) for source in range(l...  24.8 us
  transfers between devices with their start and end apart: 8, of which 8 were waited for; matrix products, arithmetic and copies ran while one was open for 0% of the time, Pallas kernels for 0%

commit v1 on v0

--- a/solution.py
+++ b/solution.py
@@ -67,7 +67,11 @@
 def on_device(slowness, freq_index, taps, source_top, adjoint_source):
     steps = slowness.shape[0]
     lines, cells = (source_top.shape[3], source_top.shape[4])
-    whole = lax.all_gather(slowness, "freq", axis=1, tiled=True).reshape(steps, lines, cells)
+    groups = lax.axis_size("freq")
+    block = slowness.shape[1]
+    spread = jnp.broadcast_to(slowness.reshape(1, steps * block), (groups, steps * block))
+    whole = lax.all_to_all(spread, "freq", 0, 0, tiled=True)
+    whole = whole.reshape(groups, steps, block).swapaxes(0, 1).reshape(steps, lines, cells)
     count = taps.shape[0]
     lanes = freq_index.shape[0]
     onehot = (freq_index[:, None] == jnp.arange(count, dtype=jnp.int32)[None, :]).astype(
@@ -118,10 +122,9 @@
     _, image = sweep(
         received, adj_re, adj_im, wave_re, wave_im, phase_cos, phase_sin, tap_re, tap_im, angular
     )
-    summed = lax.psum_scatter(
-        image.reshape(steps, lines * cells), "freq", scatter_dimension=1, tiled=True
-    )
-    return summed / count
+    parts = image.reshape(steps, groups, block).swapaxes(0, 1).reshape(groups, steps * block)
+    parts = lax.all_to_all(parts, "freq", 0, 0, tiled=True)
+    return jnp.sum(parts, axis=0).reshape(steps, block) / count
 
 
 def solution(mesh):

time: 1170 us -> 164 us (0.14)
  the two profiles are of different devices: /device:TPU:24 before, /device:TPU:1 now
where the time goes in v1:
time: 164 us; the launch traced here: 163 us
  waiting for transfers between devices  58.7 us (36%)
  starting transfers between devices  40.7 us (25%)
  other arithmetic  35.8 us (22%)
  blocking collectives  22.3 us (14%)
  local copies, waits for them, and re-layouts  4.91 us (3%)
    ppermute x7, waiting for transfers between devices, from_behind(): lax.ppermute(value, axis, [(source, source + steps) for source in range(l...  48.7 us
    all_to_all x1, starting transfers between devices, on_device(): whole = lax.all_to_all(spread, 'freq', 0, 0, tiled=True)  25 us
    all_to_all x1, blocking collectives, on_device(): parts = lax.all_to_all(parts, 'freq', 0, 0, tiled=True)  22.3 us
    another operation x21, other arithmetic, sweep(): return (jnp.stack(carry, axis=1), jnp.stack(terms))  16 us
    ppermute x7, starting transfers between devices, from_behind(): lax.ppermute(value, axis, [(source, source + steps) for source in range(l...  15.7 us
    all_to_all x1, waiting for transfers between devices, on_device(): whole = lax.all_to_all(spread, 'freq', 0, 0, tiled=True)  10 us
    add x7, other arithmetic, adjoint_step(): mid_re = phase_cos * field_re + phase_sin * field_im  5.67 us
    add x7, other arithmetic, convolve(): out_re = out_re + coef_re * shifted_re + coef_im * shifted_im  4.55 us
  transfers between devices with their start and end apart: 8, of which 8 were waited for; matrix products, arithmetic and copies ran while one was open for 2% of the time, Pallas kernels for 0%

profile of v1, /device:TPU:1, one launch (start us, length us, event | category | flops | bytes accessed | tf_op | source)
XLA Modules:
  0.0 163.0 jit_solution(12523117313550068275)
XLA Ops:
  0.0 0.7 copy-done.2
  0.7 0.7 broadcast_in_dim.5
  1.4 25.0 %all-to-all-start = ((f32[96,1,256]{2,1,0:T(1,128)}), f32[96,1,256]{2,1,0:T(1,128)S(1)}, u32[]{:S(2)}, u32[]{:S(2)}) async-start(f32[96,1,256]{2,1,0:T(1,128)} %broadcast_in_dim.5), calls=%async_computation | async-start | bytes 196608 | tf_op jit(solution)/shard_map/all_to_all | solution.py:73
  26.4 0.7 copy.20
  27.1 0.6 copy-done.3
  28.0 1.0 copy-done.1
  29.0 0.3 slice_reduce_fusion.20
  29.4 0.3 slice_reduce_fusion.21
  29.7 1.1 multiply_subtract_fusion.1
  31.0 1.1 multiply_add_fusion.1
  32.2 10.0 %all-to-all-done = f32[96,1,256]{2,1,0:T(1,128)S(1)} async-done(((f32[96,1,256]{2,1,0:T(1,128)}), f32[96,1,256]{2,1,0:T(1,128)S(1)}, u32[]{:S(2)}, u32[]{:S(2)}) %all-to-all-start) | async-done | bytes 98336 | tf_op jit(solution)/shard_map/all_to_all | solution.py:73
  42.5 95.6 %while.14 = (s32[]{:T(128)}, f32[2,2,24,1024]{3,2,0,1:T(8,128)S(1)}, f32[2,11]{0,1:T(8,128)S(1)}, f32[2,1,1,24,1024]{4,3,0,2,1:T(8,128)S(1)}, f32[2,1,1,24,1024]...) while((s32[]{:T(128)}, ...), condition=%wide.region_1.2_spmd.clone.clone, body=%wide.region_0.1_spmd.clone.clone.sunk | while | flops 8994818 | bytes 5997741 | solution.py:119
  42.5 0.8 fusion.30
  43.4 0.6 multiply_add_fusion.3
  44.0 0.6 multiply_subtract_fusion.3
  44.7 1.1 subtract_bitcast_fusion.2
  45.8 1.1 add_bitcast_fusion.2
  47.0 4.2 %collective-permute-start = (f32[2,2,24,1024]{3,2,0,1:T(8,128)S(1)}, f32[2,2,24,1024]{3,2,0,1:T(8,128)S(1)}, u32[]{:S(2)}, u32[]{:S(2)}) collective-permute-start(f32[2,2,24,1024]{3,2,0,1:T(8,128)S(1)} %pad_maximum_fusion.2), channel_id=1, source_target_pairs={{1,0},{2,1},{3,2},{4,3},{5,4},{6,5},{7,6},{9,8},{10,9},{11,10},{12... | collective-permute-start | bytes 1179656 | tf_op jit(solution)/shard_map/while/body/eval_jaxpr/ppermute | solution.py:10
  51.1 5.7 %collective-permute-done = f32[2,2,24,1024]{3,2,0,1:T(8,128)S(1)} collective-permute-done((f32[2,2,24,1024]{3,2,0,1:T(8,128)S(1)}, f32[2,2,24,1024]{3,2,0,1:T(8,128)S(1)}, u32[]{:S(2)}, u32[]{:S(2)}) %collective-permute-start) | collective-permute-done | bytes 393248 | tf_op jit(solution)/shard_map/while/body/eval_jaxpr/ppermute | solution.py:10
  56.9 0.8 fusion.30
  57.7 0.6 multiply_add_fusion.3
  58.3 0.6 multiply_subtract_fusion.3
  59.0 1.1 subtract_bitcast_fusion.2
  60.1 1.1 add_bitcast_fusion.2
  61.3 1.9 %collective-permute-start = (f32[2,2,24,1024]{3,2,0,1:T(8,128)S(1)}, f32[2,2,24,1024]{3,2,0,1:T(8,128)S(1)}, u32[]{:S(2)}, u32[]{:S(2)}) collective-permute-start(f32[2,2,24,1024]{3,2,0,1:T(8,128)S(1)} %pad_maximum_fusion.2), channel_id=1, source_target_pairs={{1,0},{2,1},{3,2},{4,3},{5,4},{6,5},{7,6},{9,8},{10,9},{11,10},{12... | collective-permute-start | bytes 1179656 | tf_op jit(solution)/shard_map/while/body/eval_jaxpr/ppermute | solution.py:10
  63.2 7.2 %collective-permute-done = f32[2,2,24,1024]{3,2,0,1:T(8,128)S(1)} collective-permute-done((f32[2,2,24,1024]{3,2,0,1:T(8,128)S(1)}, f32[2,2,24,1024]{3,2,0,1:T(8,128)S(1)}, u32[]{:S(2)}, u32[]{:S(2)}) %collective-permute-start) | collective-permute-done | bytes 393248 | tf_op jit(solution)/shard_map/while/body/eval_jaxpr/ppermute | solution.py:10
  70.4 0.8 fusion.30
  71.2 0.6 multiply_add_fusion.3
  71.9 0.6 multiply_subtract_fusion.3
  72.5 1.1 subtract_bitcast_fusion.2
  73.7 1.1 add_bitcast_fusion.2
  74.8 1.9 %collective-permute-start = (f32[2,2,24,1024]{3,2,0,1:T(8,128)S(1)}, f32[2,2,24,1024]{3,2,0,1:T(8,128)S(1)}, u32[]{:S(2)}, u32[]{:S(2)}) collective-permute-start(f32[2,2,24,1024]{3,2,0,1:T(8,128)S(1)} %pad_maximum_fusion.2), channel_id=1, source_target_pairs={{1,0},{2,1},{3,2},{4,3},{5,4},{6,5},{7,6},{9,8},{10,9},{11,10},{12... | collective-permute-start | bytes 1179656 | tf_op jit(solution)/shard_map/while/body/eval_jaxpr/ppermute | solution.py:10
  76.8 7.2 %collective-permute-done = f32[2,2,24,1024]{3,2,0,1:T(8,128)S(1)} collective-permute-done((f32[2,2,24,1024]{3,2,0,1:T(8,128)S(1)}, f32[2,2,24,1024]{3,2,0,1:T(8,128)S(1)}, u32[]{:S(2)}, u32[]{:S(2)}) %collective-permute-start) | collective-permute-done | bytes 393248 | tf_op jit(solution)/shard_map/while/body/eval_jaxpr/ppermute | solution.py:10
  83.9 0.8 fusion.30
  84.8 0.6 multiply_add_fusion.3
  85.4 0.6 multiply_subtract_fusion.3
  86.1 1.1 subtract_bitcast_fusion.2
  87.2 1.1 add_bitcast_fusion.2
  88.4 1.9 %collective-permute-start = (f32[2,2,24,1024]{3,2,0,1:T(8,128)S(1)}, f32[2,2,24,1024]{3,2,0,1:T(8,128)S(1)}, u32[]{:S(2)}, u32[]{:S(2)}) collective-permute-start(f32[2,2,24,1024]{3,2,0,1:T(8,128)S(1)} %pad_maximum_fusion.2), channel_id=1, source_target_pairs={{1,0},{2,1},{3,2},{4,3},{5,4},{6,5},{7,6},{9,8},{10,9},{11,10},{12... | collective-permute-start | bytes 1179656 | tf_op jit(solution)/shard_map/while/body/eval_jaxpr/ppermute | solution.py:10
  90.3 7.2 %collective-permute-done = f32[2,2,24,1024]{3,2,0,1:T(8,128)S(1)} collective-permute-done((f32[2,2,24,1024]{3,2,0,1:T(8,128)S(1)}, f32[2,2,24,1024]{3,2,0,1:T(8,128)S(1)}, u32[]{:S(2)}, u32[]{:S(2)}) %collective-permute-start) | collective-permute-done | bytes 393248 | tf_op jit(solution)/shard_map/while/body/eval_jaxpr/ppermute | solution.py:10
  97.5 0.8 fusion.30
  98.3 0.6 multiply_add_fusion.3
  98.9 0.6 multiply_subtract_fusion.3
  99.6 1.1 subtract_bitcast_fusion.2
  100.7 1.1 add_bitcast_fusion.2
  101.9 1.9 %collective-permute-start = (f32[2,2,24,1024]{3,2,0,1:T(8,128)S(1)}, f32[2,2,24,1024]{3,2,0,1:T(8,128)S(1)}, u32[]{:S(2)}, u32[]{:S(2)}) collective-permute-start(f32[2,2,24,1024]{3,2,0,1:T(8,128)S(1)} %pad_maximum_fusion.2), channel_id=1, source_target_pairs={{1,0},{2,1},{3,2},{4,3},{5,4},{6,5},{7,6},{9,8},{10,9},{11,10},{12... | collective-permute-start | bytes 1179656 | tf_op jit(solution)/shard_map/while/body/eval_jaxpr/ppermute | solution.py:10
  103.8 7.2 %collective-permute-done = f32[2,2,24,1024]{3,2,0,1:T(8,128)S(1)} collective-permute-done((f32[2,2,24,1024]{3,2,0,1:T(8,128)S(1)}, f32[2,2,24,1024]{3,2,0,1:T(8,128)S(1)}, u32[]{:S(2)}, u32[]{:S(2)}) %collective-permute-start) | collective-permute-done | bytes 393248 | tf_op jit(solution)/shard_map/while/body/eval_jaxpr/ppermute | solution.py:10
  111.0 0.8 fusion.30
  111.8 0.6 multiply_add_fusion.3
  112.5 0.6 multiply_subtract_fusion.3
  113.1 1.1 subtract_bitcast_fusion.2
  114.3 1.1 add_bitcast_fusion.2
  115.4 1.9 %collective-permute-start = (f32[2,2,24,1024]{3,2,0,1:T(8,128)S(1)}, f32[2,2,24,1024]{3,2,0,1:T(8,128)S(1)}, u32[]{:S(2)}, u32[]{:S(2)}) collective-permute-start(f32[2,2,24,1024]{3,2,0,1:T(8,128)S(1)} %pad_maximum_fusion.2), channel_id=1, source_target_pairs={{1,0},{2,1},{3,2},{4,3},{5,4},{6,5},{7,6},{9,8},{10,9},{11,10},{12... | collective-permute-start | bytes 1179656 | tf_op jit(solution)/shard_map/while/body/eval_jaxpr/ppermute | solution.py:10
  117.4 7.2 %collective-permute-done = f32[2,2,24,1024]{3,2,0,1:T(8,128)S(1)} collective-permute-done((f32[2,2,24,1024]{3,2,0,1:T(8,128)S(1)}, f32[2,2,24,1024]{3,2,0,1:T(8,128)S(1)}, u32[]{:S(2)}, u32[]{:S(2)}) %collective-permute-start) | collective-permute-done | bytes 393248 | tf_op jit(solution)/shard_map/while/body/eval_jaxpr/ppermute | solution.py:10
  124.5 0.8 fusion.30
  125.4 0.6 multiply_add_fusion.3
  126.0 0.6 multiply_subtract_fusion.3
  126.7 1.1 subtract_bitcast_fusion.2
  127.8 1.1 add_bitcast_fusion.2
  129.0 1.9 %collective-permute-start = (f32[2,2,24,1024]{3,2,0,1:T(8,128)S(1)}, f32[2,2,24,1024]{3,2,0,1:T(8,128)S(1)}, u32[]{:S(2)}, u32[]{:S(2)}) collective-permute-start(f32[2,2,24,1024]{3,2,0,1:T(8,128)S(1)} %pad_maximum_fusion.2), channel_id=1, source_target_pairs={{1,0},{2,1},{3,2},{4,3},{5,4},{6,5},{7,6},{9,8},{10,9},{11,10},{12... | collective-permute-start | bytes 1179656 | tf_op jit(solution)/shard_map/while/body/eval_jaxpr/ppermute | solution.py:10
  130.9 7.2 %collective-permute-done = f32[2,2,24,1024]{3,2,0,1:T(8,128)S(1)} collective-permute-done((f32[2,2,24,1024]{3,2,0,1:T(8,128)S(1)}, f32[2,2,24,1024]{3,2,0,1:T(8,128)S(1)}, u32[]{:S(2)}, u32[]{:S(2)}) %collective-permute-start) | collective-permute-done | bytes 393248 | tf_op jit(solution)/shard_map/while/body/eval_jaxpr/ppermute | solution.py:10
  138.1 1.9 %fusion.20 = f32[24,1024]{1,0:T(8,128)S(1)} fusion(f32[2,2,24,1024]{3,2,0,1:T(8,128)S(1)} %get-tuple-element.106, f32[2,24,1024]{2,1,0:T(8,128)S(1)} %multiply_subtract_fusion.1, f32[2,24,1024]{2,1,0:T(8,128)S(1)} %multiply_add_fusion.1, f32[2,1,2,24,1024]{4,3,2,1,0:T(8,128)S(1)} %copy-done, f32[2]{0:T(128)S(1)} %get-tuple-element.193, ...), kind=kLoop, calls=%fused_computation.131 | loop fusion | flops 4890624 | bytes 1376440 | tf_op jit(solution)/shard_map/reduce_sum | solution.py:60
  140.1 22.3 %all_to_all.15 = f32[96,1,256]{2,1,0:T(1,128)S(1)} all-to-all(f32[96,1,256]{2,1,0:T(1,128)S(1)} %all_to_all.11), channel_id=1, replica_groups=mesh['freq'=96,'depth'=8] {'freq'}, dimensions={0} | all-to-all | bytes 196608 | tf_op jit(solution)/shard_map/all_to_all | solution.py:126
  162.4 0.6 broadcast_multiply_fusion
  (40 shorter events, 1.3 us)
Async XLA Ops:
  0.0 0.7 copy-start.2
  0.0 27.9 %copy-start = (f32[2,1,2,24,1024]{4,3,2,1,0:T(8,128)S(1)}, f32[2,1,2,24,1024]{4,3,2,1,0:T(8,128)}, u32[]{:S(2)}) copy-start(f32[2,1,2,24,1024]{4,3,2,1,0:T(8,128)} %param.11) | copy-start | bytes 1179652
  1.4 40.8 %all-to-all-start = ((f32[96,1,256]{2,1,0:T(1,128)}), f32[96,1,256]{2,1,0:T(1,128)S(1)}, u32[]{:S(2)}, u32[]{:S(2)}) async-start(f32[96,1,256]{2,1,0:T(1,128)} %broadcast_in_dim.5), calls=%async_computation | async-start | bytes 196608 | tf_op jit(solution)/shard_map/all_to_all | solution.py:73
  27.1 0.7 copy-start.3
  28.0 1.0 copy-start.1
  47.0 9.9 %collective-permute-start = (f32[2,2,24,1024]{3,2,0,1:T(8,128)S(1)}, f32[2,2,24,1024]{3,2,0,1:T(8,128)S(1)}, u32[]{:S(2)}, u32[]{:S(2)}) collective-permute-start(f32[2,2,24,1024]{3,2,0,1:T(8,128)S(1)} %pad_maximum_fusion.2), channel_id=1, source_target_pairs={{1,0},{2,1},{3,2},{4,3},{5,4},{6,5},{7,6},{9,8},{10,9},{11,10},{12... | collective-permute-start | bytes 1179656 | tf_op jit(solution)/shard_map/while/body/eval_jaxpr/ppermute | solution.py:10
  61.3 9.1 %collective-permute-start = (f32[2,2,24,1024]{3,2,0,1:T(8,128)S(1)}, f32[2,2,24,1024]{3,2,0,1:T(8,128)S(1)}, u32[]{:S(2)}, u32[]{:S(2)}) collective-permute-start(f32[2,2,24,1024]{3,2,0,1:T(8,128)S(1)} %pad_maximum_fusion.2), channel_id=1, source_target_pairs={{1,0},{2,1},{3,2},{4,3},{5,4},{6,5},{7,6},{9,8},{10,9},{11,10},{12... | collective-permute-start | bytes 1179656 | tf_op jit(solution)/shard_map/while/body/eval_jaxpr/ppermute | solution.py:10
  74.8 9.1 %collective-permute-start = (f32[2,2,24,1024]{3,2,0,1:T(8,128)S(1)}, f32[2,2,24,1024]{3,2,0,1:T(8,128)S(1)}, u32[]{:S(2)}, u32[]{:S(2)}) collective-permute-start(f32[2,2,24,1024]{3,2,0,1:T(8,128)S(1)} %pad_maximum_fusion.2), channel_id=1, source_target_pairs={{1,0},{2,1},{3,2},{4,3},{5,4},{6,5},{7,6},{9,8},{10,9},{11,10},{12... | collective-permute-start | bytes 1179656 | tf_op jit(solution)/shard_map/while/body/eval_jaxpr/ppermute | solution.py:10
  88.4 9.1 %collective-permute-start = (f32[2,2,24,1024]{3,2,0,1:T(8,128)S(1)}, f32[2,2,24,1024]{3,2,0,1:T(8,128)S(1)}, u32[]{:S(2)}, u32[]{:S(2)}) collective-permute-start(f32[2,2,24,1024]{3,2,0,1:T(8,128)S(1)} %pad_maximum_fusion.2), channel_id=1, source_target_pairs={{1,0},{2,1},{3,2},{4,3},{5,4},{6,5},{7,6},{9,8},{10,9},{11,10},{12... | collective-permute-start | bytes 1179656 | tf_op jit(solution)/shard_map/while/body/eval_jaxpr/ppermute | solution.py:10
  101.9 9.1 %collective-permute-start = (f32[2,2,24,1024]{3,2,0,1:T(8,128)S(1)}, f32[2,2,24,1024]{3,2,0,1:T(8,128)S(1)}, u32[]{:S(2)}, u32[]{:S(2)}) collective-permute-start(f32[2,2,24,1024]{3,2,0,1:T(8,128)S(1)} %pad_maximum_fusion.2), channel_id=1, source_target_pairs={{1,0},{2,1},{3,2},{4,3},{5,4},{6,5},{7,6},{9,8},{10,9},{11,10},{12... | collective-permute-start | bytes 1179656 | tf_op jit(solution)/shard_map/while/body/eval_jaxpr/ppermute | solution.py:10
  115.4 9.1 %collective-permute-start = (f32[2,2,24,1024]{3,2,0,1:T(8,128)S(1)}, f32[2,2,24,1024]{3,2,0,1:T(8,128)S(1)}, u32[]{:S(2)}, u32[]{:S(2)}) collective-permute-start(f32[2,2,24,1024]{3,2,0,1:T(8,128)S(1)} %pad_maximum_fusion.2), channel_id=1, source_target_pairs={{1,0},{2,1},{3,2},{4,3},{5,4},{6,5},{7,6},{9,8},{10,9},{11,10},{12... | collective-permute-start | bytes 1179656 | tf_op jit(solution)/shard_map/while/body/eval_jaxpr/ppermute | solution.py:10
  129.0 9.1 %collective-permute-start = (f32[2,2,24,1024]{3,2,0,1:T(8,128)S(1)}, f32[2,2,24,1024]{3,2,0,1:T(8,128)S(1)}, u32[]{:S(2)}, u32[]{:S(2)}) collective-permute-start(f32[2,2,24,1024]{3,2,0,1:T(8,128)S(1)} %pad_maximum_fusion.2), channel_id=1, source_target_pairs={{1,0},{2,1},{3,2},{4,3},{5,4},{6,5},{7,6},{9,8},{10,9},{11,10},{12... | collective-permute-start | bytes 1179656 | tf_op jit(solution)/shard_map/while/body/eval_jaxpr/ppermute | solution.py:10

commit v2 on v0

v2 whole, which is shorter than its diff:
```python
import functools
import jax
import jax.numpy as jnp
from jax import lax
from jax.experimental import pallas as pl
from jax.experimental.pallas import tpu as pltpu
from jax.sharding import PartitionSpec as P

CORES = 2
MARGIN = 64
VMEM = pl.BlockSpec(memory_space=pltpu.VMEM)
SMEM = pl.BlockSpec(memory_space=pltpu.SMEM)


def call(kernel, outs, in_specs, scratch=(), flops=0, moved=0):
    shapes = [jax.ShapeDtypeStruct(s, jnp.float32) for s in outs]
    return pl.pallas_call(
        kernel,
        out_shape=shapes if len(shapes) > 1 else shapes[0],
        in_specs=in_specs,
        out_specs=[VMEM] * len(shapes) if len(shapes) > 1 else VMEM,
        scratch_shapes=list(scratch),
        compiler_params=pltpu.CompilerParams(vmem_limit_bytes=40 << 20),
        cost_estimate=pl.CostEstimate(flops=flops, bytes_accessed=moved, transcendentals=0),
    )


def sincos(x):
    k = jnp.floor(x * 0.6366197723675814 + 0.5)
    r = x - k * 1.5703125
    r = r - k * 4.837512969970703e-4
    r = r - k * 7.549789948768648e-8
    r2 = r * r
    s = r + r * r2 * (-1.6666654611e-1 + r2 * (8.3321608736e-3 + r2 * -1.9515295891e-4))
    c = 1.0 - 0.5 * r2 + r2 * r2 * (
        4.166664568298827e-2 + r2 * (-1.388731625493765e-3 + r2 * 2.443315711809948e-5)
    )
    q = k.astype(jnp.int32)
    odd = (q & 1) == 1
    sin = jnp.where(odd, c, s)
    cos = jnp.where(odd, s, c)
    sin = jnp.where((q & 2) == 2, -sin, sin)
    cos = jnp.where(((q + 1) & 2) == 2, -cos, cos)
    return sin, cos


def along_x(re, im, taps, adjoint):
    width = re.shape[-1]
    count = len(taps)
    reach = count // 2
    out_re = out_im = None
    for k, (a, b) in enumerate(taps):
        shift = (reach - k) if not adjoint else (k - reach)
        s_re = pltpu.roll(re, shift % width, 1) if shift else re
        s_im = pltpu.roll(im, shift % width, 1) if shift else im
        if adjoint:
            t_re, t_im = a * s_re + b * s_im, a * s_im - b * s_re
        else:
            t_re, t_im = a * s_re - b * s_im, a * s_im + b * s_re
        out_re = t_re if out_re is None else out_re + t_re
        out_im = t_im if out_im is None else out_im + t_im
    return out_re, out_im


def along_y(ref, lines, tile, taps, adjoint):
    count = len(taps)
    reach = count // 2
    lanes = pl.ds(tile * 128, 128)
    out_re = out_im = None
    for k, (a, b) in enumerate(taps):
        first = 8 + ((k - reach) if not adjoint else (reach - k))
        s_re = ref[0, pl.ds(first, lines), lanes]
        s_im = ref[1, pl.ds(first, lines), lanes]
        if adjoint:
            t_re, t_im = a * s_re + b * s_im, a * s_im - b * s_re
        else:
            t_re, t_im = a * s_re - b * s_im, a * s_im + b * s_re
        out_re = t_re if out_re is None else out_re + t_re
        out_im = t_im if out_im is None else out_im + t_im
    return out_re, out_im


def read_taps(tap_ref, count):
    return [(tap_ref[k], tap_ref[count + k]) for k in range(count)]


def pack_kernel(quarters, where_ref, adj_ref, src_ref, got_ref, *refs):
    outs, pad_ref = refs[:-1], refs[-1]
    core, quarter = where_ref[0], where_ref[1]
    cells = adj_ref.shape[-1]
    lines = adj_ref.shape[-2]
    width = cells // quarters
    for zz in range(2):
        for n in range(4):
            pad_ref[zz, n, :, :128] = jnp.zeros((lines, 128), jnp.float32)
            pad_ref[zz, n, :, 128 + cells :] = jnp.zeros((lines, 128), jnp.float32)
    for part in range(2):
        pad_ref[core, part, :, 128 : 128 + cells] = adj_ref[core, part]
        pad_ref[core, 2 + part, :, 128 : 128 + cells] = src_ref[core, part]
        pad_ref[1 - core, part, :, 128 : 128 + cells] = got_ref[0, part]
        pad_ref[1 - core, 2 + part, :, 128 : 128 + cells] = got_ref[1, part]
    for k, out_ref in enumerate(outs):
        aim = lax.rem(quarter + k, quarters)
        lanes = pl.ds(pl.multiple_of(aim * width, 128), width + 256)
        for zz in range(2):
            for n in range(4):
                wide = pad_ref[zz, n, :, lanes]
                wide = pltpu.roll(wide, width + 256 - (128 - MARGIN), 1)
                out_ref[zz, n] = wide[:, : width + 2 * MARGIN]


def forward_kernel(quarters, count, where_ref, tap_ref, *refs):
    ins, (adj_ref, mid_ref), pad_ref = refs[:quarters], refs[quarters : quarters + 2], refs[-1]
    quarter = where_ref[1]
    taps = read_taps(tap_ref, count)
    lines, span = ins[0].shape[-2], ins[0].shape[-1]
    for part in range(2):
        pad_ref[part, :8] = jnp.zeros((8, span), jnp.float32)
        pad_ref[part, 8 + lines :] = jnp.zeros((8, span), jnp.float32)
    for k, in_ref in enumerate(ins):
        chip = lax.rem(quarter + quarters - k, quarters)
        for zz in range(2):
            z = chip * 2 + zz
            for part in range(2):
                adj_ref[z, part] = in_ref[zz, part]
            for row in range(0, lines, 8):
                rows = pl.ds(row, min(8, lines - row))
                re, im = along_x(in_ref[zz, 2, rows], in_ref[zz, 3, rows], taps, False)
                pad_ref[0, pl.ds(8 + row, re.shape[0])] = re
                pad_ref[1, pl.ds(8 + row, re.shape[0])] = im
            for tile in range(span // 128):
                re, im = along_y(pad_ref, lines, tile, taps, False)
                mid_ref[z, 0, :, tile * 128 : tile * 128 + 128] = re
                mid_ref[z, 1, :, tile * 128 : tile * 128 + 128] = im


def slow_kernel(quarters, in_ref, out_ref, pad_ref, *half_refs):
    width = in_ref.shape[-1]
    lines = in_ref.shape[0] // quarters
    cells = width * quarters
    pad_ref[:, :128] = jnp.zeros((lines, 128), jnp.float32)
    pad_ref[:, 128 + cells :] = jnp.zeros((lines, 128), jnp.float32)
    for n in range(width // 128):
        half_refs[n][...] = in_ref[:, n * 128 : n * 128 + 128]
    for c in range(quarters):
        for n in range(width // 128):
            first = 128 + c * width + n * 128
            pad_ref[:, first : first + 128] = half_refs[n][pl.ds(c, lines, stride=quarters), :]
    for c in range(quarters):
        wide = pad_ref[:, c * width : c * width + width + 256]
        wide = pltpu.roll(wide, width + 256 - (128 - MARGIN), 1)[:, : width + 2 * MARGIN]
        for core in range(CORES):
            out_ref[c * CORES + core] = wide


def chain_kernel(
    quarters, cells, count, where_ref, omega_ref, tap_ref, slow_ref, adj_ref, mid_ref, out_ref, mu_ref, pad_ref
):
    quarter = where_ref[1]
    omega = omega_ref[0]
    taps = read_taps(tap_ref, count)
    steps, lines, span = slow_ref.shape
    width = cells // quarters
    for part in range(2):
        pad_ref[part, :8] = jnp.zeros((8, span), jnp.float32)
        pad_ref[part, 8 + lines :] = jnp.zeros((8, span), jnp.float32)
        mu_ref[part] = jnp.zeros((lines, span), jnp.float32)
    for z in reversed(range(steps)):
        for row in range(0, lines, 8):
            many = min(8, lines - row)
            rows = pl.ds(row, many)
            mu_re = adj_ref[z, 0, rows] + mu_ref[0, rows]
            mu_im = adj_ref[z, 1, rows] + mu_ref[1, rows]
            sin, cos = sincos(omega * slow_ref[z, rows])
            mid_re, mid_im = mid_ref[z, 0, rows], mid_ref[z, 1, rows]
            wave_re = cos * mid_re - sin * mid_im
            wave_im = sin * mid_re + cos * mid_im
            term = omega * (mu_im * wave_re - mu_re * wave_im)
            out_ref[z, rows] = pltpu.roll(term, span - MARGIN, 1)[:, :width]
            if z:
                pad_ref[0, pl.ds(8 + row, many)] = cos * mu_re + sin * mu_im
                pad_ref[1, pl.ds(8 + row, many)] = cos * mu_im - sin * mu_re
        if z:
            for tile in range(span // 128):
                re, im = along_y(pad_ref, lines, tile, taps, True)
                mu_ref[0, :, tile * 128 : tile * 128 + 128] = re
                mu_ref[1, :, tile * 128 : tile * 128 + 128] = im
            for row in range(0, lines, 8):
                many = min(8, lines - row)
                rows = pl.ds(row, many)
                column = lax.broadcasted_iota(jnp.int32, (many, span), 1) + (quarter * width - MARGIN)
                inside = (column >= 0) & (column < cells)
                re, im = along_x(mu_ref[0, rows], mu_ref[1, rows], taps, True)
                mu_ref[0, rows] = jnp.where(inside, re, 0.0)
                mu_ref[1, rows] = jnp.where(inside, im, 0.0)


def regroup_kernel(quarters, in_ref, out_ref, *half_refs):
    lines, width = in_ref.shape[1], in_ref.shape[2]
    for c in range(quarters):
        both = in_ref[CORES * c] + in_ref[CORES * c + 1]
        for n in range(width // 128):
            half_refs[n][pl.ds(c, lines, stride=quarters), :] = both[:, n * 128 : n * 128 + 128]
    for n in range(width // 128):
        out_ref[:, n * 128 : n * 128 + 128] = half_refs[n][...]


def on_device(slowness, freq_index, taps, source_top, adjoint_source):
    lines, cells = source_top.shape[3], source_top.shape[4]
    groups, sections = lax.axis_size("freq"), lax.axis_size("depth")
    block = slowness.shape[1]
    quarters = sections // CORES
    width = cells // quarters
    span = width + 2 * MARGIN
    count, points = taps.shape[0], taps.shape[2]

    depth = lax.axis_index("depth")
    core, quarter = depth % CORES, depth // CORES
    where = jnp.stack([core, quarter]).astype(jnp.int32)
    chosen = lax.dynamic_index_in_dim(freq_index, core, 0, False)
    tap_row = lax.dynamic_index_in_dim(taps, chosen, 0, False).reshape(-1)
    omega = (8.0 * (chosen.astype(jnp.float32) + 1.0) / count).reshape(1)

    adj, src = adjoint_source[:, 0], source_top[:, 0]
    other = jnp.where(core == 0, jnp.stack([adj[1], src[1]]), jnp.stack([adj[0], src[0]]))
    got = lax.ppermute(other, "depth", [(d, d ^ 1) for d in range(sections)])

    spread = jnp.broadcast_to(slowness, (groups, block))
    plane = lax.all_to_all(spread, "freq", 0, 0, tiled=True)

    windows = call(
        functools.partial(pack_kernel, quarters),
        [(2, 4, lines, span)] * quarters,
        [SMEM, VMEM, VMEM, VMEM],
        [pltpu.VMEM((2, 4, lines, cells + 256), jnp.float32)],
        flops=1 << 20,
        moved=4 << 20,
    )(where, adj, src, got)
    arrived = [windows[0]]
    for k in range(1, quarters):
        hop = [(d, (d + CORES * k) % sections) for d in range(sections)]
        arrived.append(lax.ppermute(windows[k], "depth", hop))

    plane, *arrived = lax.optimization_barrier((plane, *arrived))
    slow = call(
        functools.partial(slow_kernel, quarters),
        [(sections, lines, span)],
        [VMEM],
        [
            pltpu.VMEM((lines, cells + 256), jnp.float32),
            *[pltpu.VMEM((groups, 128), jnp.float32)] * (block // 128),
        ],
        flops=1 << 18,
        moved=1 << 19,
    )(plane)
    slow = lax.all_to_all(slow, "depth", 0, 0, tiled=True)

    adj_all, mid_all = call(
        functools.partial(forward_kernel, quarters, points),
        [(sections, 2, lines, span)] * 2,
        [SMEM, SMEM] + [VMEM] * quarters,
        [pltpu.VMEM((2, lines + 16, span), jnp.float32)],
        flops=1 << 24,
        moved=4 << 20,
    )(where, tap_row, *arrived)

    image = call(
        functools.partial(chain_kernel, quarters, cells, points),
        [(sections, lines, width)],
        [SMEM, SMEM, SMEM, VMEM, VMEM, VMEM],
        [
            pltpu.VMEM((2, lines, span), jnp.float32),
            pltpu.VMEM((2, lines + 16, span), jnp.float32),
        ],
        flops=1 << 25,
        moved=4 << 20,
    )(where, omega, tap_row, slow, adj_all, mid_all)

    image = lax.all_to_all(image, "depth", 0, 0, tiled=True)
    rows = call(
        functools.partial(regroup_kernel, quarters),
        [(groups, block)],
        [VMEM],
        [pltpu.VMEM((groups, 128), jnp.float32)] * (block // 128),
        flops=1 << 17,
        moved=1 << 19,
    )(image)
    rows = lax.all_to_all(rows, "freq", 0, 0, tiled=True)
    return jnp.sum(rows, axis=0, keepdims=True) / count


def solution(mesh):
    in_specs = (
        P("depth", "freq"),
        P("freq"),
        P(),
        P("freq", "depth", None, None, None),
        P("freq", "depth", None, None, None),
    )
    out_specs = P("depth", "freq")
    return jax.shard_map(
        on_device, mesh=mesh, in_specs=in_specs, out_specs=out_specs, check_vma=False
    )
```

time: 1170 us -> 109 us (0.09)
  the two profiles are of different devices: /device:TPU:24 before, /device:TPU:1 now
where the time goes in v2:
time: 109 us; the launch traced here: 108 us
  blocking collectives  61.9 us (57%)
  starting transfers between devices  27.4 us (25%)
  Pallas kernels  8.74 us (8%)
  waiting for transfers between devices  3.27 us (3%)
  local copies, waits for them, and re-layouts  2.97 us (3%)
  between operations  2.75 us (3%)
    all_to_all x1, blocking collectives, on_device(): plane = lax.all_to_all(spread, 'freq', 0, 0, tiled=True)  30.8 us
    all_to_all x1, blocking collectives, on_device(): rows = lax.all_to_all(rows, 'freq', 0, 0, tiled=True)  21.2 us
    ppermute x1, starting transfers between devices, on_device(): got = lax.ppermute(other, 'depth', [(d, d ^ 1) for d in range(sections)])  12.6 us
    all_to_all x1, blocking collectives, on_device(): image = lax.all_to_all(image, 'depth', 0, 0, tiled=True)  9.93 us
    ppermute x3, starting transfers between devices, on_device(): arrived.append(lax.ppermute(windows[k], 'depth', hop))  9 us
    all_to_all x1, starting transfers between devices, on_device(): slow = lax.all_to_all(slow, 'depth', 0, 0, tiled=True)  5.8 us
    pallas_call x1, Pallas kernels, on_device(): call(functools.partial(chain_kernel, quarters, cells, points), [(sections...  3.57 us
    pallas_call x1, Pallas kernels, on_device(): call(functools.partial(forward_kernel, quarters, points), [(sections, 2,...  3.25 us
  transfers between devices with their start and end apart: 5, of which 2 were waited for; matrix products, arithmetic and copies ran while one was open for 1% of the time, Pallas kernels for 3%

profile of v2, /device:TPU:1, one launch (start us, length us, event | category | flops | bytes accessed | tf_op | source)
XLA Modules:
  0.0 107.8 jit_solution(5360203583489560440)
XLA Ops:
  0.0 0.0 copy-start
  0.0 1.3 %slice_bitcast_fusion = (f32[1,2,24,1024]{3,2,1,0:T(8,128)S(1)}, f32[1,2,24,1024]{3,2,1,0:T(8,128)S(1)}, f32[1,2,24,1024]{3,2,1,0:T(8,128)S(1)}, f32[1,2,24,1024]{3,2,1,0:T(8,128)S(1)}) fusion(f32[2,1,2,24,1024]{4,3,2,1,0:T(8,128)} %param.8, f32[2,1,2,24,1024]{4,3,2,1,0:T(8,128)} %param.9), kind=kLoop, calls=%fused_computation.1 | loop fusion | bytes 1572864 | tf_op jit(solution)/shard_map/slice | solution.py:225
  1.3 0.0 copy-start.1
  1.3 0.0 copy-start.2
  1.4 12.6 %collective-permute-start = (f32[2,2,24,1024]{3,2,1,0:T(8,128)S(1)}, f32[2,2,24,1024]{3,2,1,0:T(8,128)S(1)}, u32[]{:S(2)}, u32[]{:S(2)}) collective-permute-start(f32[2,2,24,1024]{3,2,1,0:T(8,128)S(1)} %maximum_select_fusion), channel_id=1, source_target_pairs={{0,1},{1,0},{2,3},{3,2},{4,5},{5,4},{6,7},{7,6},{8,9},{9,8},{10,11... | collective-permute-start | bytes 1179656 | tf_op jit(solution)/shard_map/ppermute | solution.py:226
  13.9 0.1 pad_add_fusion.where_ref
  14.0 1.2 %collective-permute-done.got_ref = f32[2,2,24,1024]{3,2,1,0:T(8,128)S(1)} collective-permute-done((f32[2,2,24,1024]{3,2,1,0:T(8,128)S(1)}, f32[2,2,24,1024]{3,2,1,0:T(8,128)S(1)}, u32[]{:S(2)}, u32[]{:S(2)}) %collective-permute-start) | collective-permute-done | bytes 393248 | tf_op jit(solution)/shard_map/ppermute | solution.py:226
  15.3 0.0 copy-done.1
  15.3 0.0 copy-done.2
  15.3 1.1 shard_map.58
  16.3 1.9 %collective-permute-start.1 = (f32[2,4,24,384]{3,2,1,0:T(8,128)S(1)}, f32[2,4,24,384]{3,2,1,0:T(8,128)S(1)}, u32[]{:S(2)}, u32[]{:S(2)}) collective-permute-start(f32[2,4,24,384]{3,2,1,0:T(8,128)S(1)} %get-tuple-element.17), channel_id=1, source_target_pairs={{0,2},{1,3},{2,4},{3,5},{4,6},{5,7},{6,0},{7,1},{8,10},{9,11},{10,... | collective-permute-start | bytes 884744 | tf_op jit(solution)/shard_map/ppermute | solution.py:242
  18.3 1.9 %collective-permute-start.2 = (f32[2,4,24,384]{3,2,1,0:T(8,128)S(1)}, f32[2,4,24,384]{3,2,1,0:T(8,128)S(1)}, u32[]{:S(2)}, u32[]{:S(2)}) collective-permute-start(f32[2,4,24,384]{3,2,1,0:T(8,128)S(1)} %get-tuple-element.18), channel_id=1, source_target_pairs={{0,4},{1,5},{2,6},{3,7},{4,0},{5,1},{6,2},{7,3},{8,12},{9,13},{10,... | collective-permute-start | bytes 884744 | tf_op jit(solution)/shard_map/ppermute | solution.py:242
  20.2 0.0 copy-start.3
  20.2 5.2 %collective-permute-start.3 = (f32[2,4,24,384]{3,2,1,0:T(8,128)S(1)}, f32[2,4,24,384]{3,2,1,0:T(8,128)S(1)}, u32[]{:S(2)}, u32[]{:S(2)}) collective-permute-start(f32[2,4,24,384]{3,2,1,0:T(8,128)S(1)} %get-tuple-element.19), channel_id=1, source_target_pairs={{0,6},{1,7},{2,0},{3,1},{4,2},{5,3},{6,4},{7,5},{8,14},{9,15},{10,... | collective-permute-start | bytes 884744 | tf_op jit(solution)/shard_map/ppermute | solution.py:242
  25.4 0.0 copy-done.3
  25.4 0.1 broadcast_in_dim.2
  25.4 30.8 %all_to_all.28 = f32[96,1,256]{2,1,0:T(1,128)S(1)} all-to-all(f32[96,1,256]{2,1,0:T(1,128)S(1)} %broadcast_in_dim.2), channel_id=1, replica_groups=mesh['freq'=96,'depth'=8] {'freq'}, dimensions={0} | all-to-all | bytes 196608 | tf_op jit(solution)/shard_map/all_to_all | solution.py:229
  56.3 0.0 collective-permute-done.1.refs_1_
  56.3 0.0 collective-permute-done.2.refs_2_
  56.3 0.0 collective-permute-done.3.refs_3_
  56.3 0.8 shard_map.59
  57.1 5.8 %all-to-all-start.1 = ((f32[8,24,384]{2,1,0:T(8,128)}), f32[8,24,384]{2,1,0:T(8,128)S(1)}, u32[]{:S(2)}, u32[]{:S(2)}) async-start(f32[8,24,384]{2,1,0:T(8,128)} %shard_map.59), calls=%async_computation.1 | async-start | bytes 589824 | tf_op jit(solution)/shard_map/all_to_all | solution.py:256
  62.9 0.0 copy-start.4
  62.9 0.7 copy-done.4
  63.6 0.6 dynamic_slice.8
  66.7 0.0 copy-done
  66.7 0.1 constant_dynamic-slice_fusion
  66.8 0.1 copy.7
  66.9 0.1 reshape.30.tap_ref
  67.0 3.2 %shard_map.60 = (f32[8,2,24,384]{3,2,1,0:T(8,128)S(1)}, f32[8,2,24,384]{3,2,1,0:T(8,128)S(1)}) custom-call(s32[2]{0:T(128)S(1)} %pad_add_fusion.where_ref, f32[22]{0:T(128)S(1)} %reshape.30.tap_ref, f32[2,4,24,384]{3,2,1,0:T(8,128)S(1)} %get-tuple-element.21.refs_0_, f32[2,4,24,384]{3,2,1,0:T(8,128)S(1)} %collective-permute-done.1.refs_1_, ...), custom_call_target="tpu_custom_call" | custom-call | flops 16777216 | bytes 4194304 | tf_op jit(solution)/shard_map/pallas_call | solution.py:258
  70.3 2.0 %all-to-all-done.1.slow_ref = f32[8,24,384]{2,1,0:T(8,128)S(1)} async-done(((f32[8,24,384]{2,1,0:T(8,128)}), f32[8,24,384]{2,1,0:T(8,128)S(1)}, u32[]{:S(2)}, u32[]{:S(2)}) %all-to-all-start.1) | async-done | bytes 294944 | tf_op jit(solution)/shard_map/all_to_all | solution.py:256
  72.3 3.6 %shard_map.61 = f32[8,24,256]{2,1,0:T(8,128)S(1)} custom-call(s32[2]{0:T(128)S(1)} %pad_add_fusion.where_ref, f32[1]{0:T(128)} %bitcast.3.omega_ref, f32[22]{0:T(128)S(1)} %reshape.30.tap_ref, f32[8,24,384]{2,1,0:T(8,128)S(1)} %all-to-all-done.1.slow_ref, f32[8,2,24,384]{3,2,1,0:T(8,128)S(1)} %get-tuple-element.25.adj_ref, ...), custom_call_target="tpu_custom_call" | custom-call | flops 33554432 | bytes 4194304 | tf_op jit(solution)/shard_map/pallas_call | solution.py:267
  75.9 9.9 %all_to_all.29.in_ref = f32[8,24,256]{2,1,0:T(8,128)S(1)} all-to-all(f32[8,24,256]{2,1,0:T(8,128)S(1)} %shard_map.61), channel_id=1, replica_groups=mesh['freq'=96,'depth'=8] {'depth'}, dimensions={0} | all-to-all | bytes 393216 | tf_op jit(solution)/shard_map/all_to_all | solution.py:279
  85.8 0.1 copy.8
  85.9 21.2 %all_to_all.30 = f32[96,1,256]{2,1,0:T(1,128)S(1)} all-to-all(f32[96,1,256]{2,1,0:T(1,128)S(1)} %copy.8), channel_id=1, replica_groups=mesh['freq'=96,'depth'=8] {'freq'}, dimensions={0} | all-to-all | bytes 196608 | tf_op jit(solution)/shard_map/all_to_all | solution.py:288
  107.1 0.1 reduce_sum.9
  107.2 0.6 broadcast_multiply_fusion
  (3 shorter events, 0.1 us)
Async XLA Ops:
  0.0 66.7 %copy-start = (f32[192,2,11]{0,1,2:T(2,128)S(1)}, f32[192,2,11]{0,1,2:T(2,128)}, u32[]{:S(2)}) copy-start(f32[192,2,11]{0,1,2:T(2,128)} %param.7) | copy-start | bytes 50692
  1.3 14.0 %copy-start.1 = (f32[2,1,2,24,1024]{4,3,2,1,0:T(8,128)S(1)}, f32[2,1,2,24,1024]{4,3,2,1,0:T(8,128)}, u32[]{:S(2)}) copy-start(f32[2,1,2,24,1024]{4,3,2,1,0:T(8,128)} %param.9) | copy-start | bytes 1179652
  1.3 14.0 %copy-start.2 = (f32[2,1,2,24,1024]{4,3,2,1,0:T(8,128)S(1)}, f32[2,1,2,24,1024]{4,3,2,1,0:T(8,128)}, u32[]{:S(2)}) copy-start(f32[2,1,2,24,1024]{4,3,2,1,0:T(8,128)} %param.8) | copy-start | bytes 1179652
  1.4 13.9 %collective-permute-start = (f32[2,2,24,1024]{3,2,1,0:T(8,128)S(1)}, f32[2,2,24,1024]{3,2,1,0:T(8,128)S(1)}, u32[]{:S(2)}, u32[]{:S(2)}) collective-permute-start(f32[2,2,24,1024]{3,2,1,0:T(8,128)S(1)} %maximum_select_fusion), channel_id=1, source_target_pairs={{0,1},{1,0},{2,3},{3,2},{4,5},{5,4},{6,7},{7,6},{8,9},{9,8},{10,11... | collective-permute-start | bytes 1179656 | tf_op jit(solution)/shard_map/ppermute | solution.py:226
  16.3 39.9 %collective-permute-start.1 = (f32[2,4,24,384]{3,2,1,0:T(8,128)S(1)}, f32[2,4,24,384]{3,2,1,0:T(8,128)S(1)}, u32[]{:S(2)}, u32[]{:S(2)}) collective-permute-start(f32[2,4,24,384]{3,2,1,0:T(8,128)S(1)} %get-tuple-element.17), channel_id=1, source_target_pairs={{0,2},{1,3},{2,4},{3,5},{4,6},{5,7},{6,0},{7,1},{8,10},{9,11},{10,... | collective-permute-start | bytes 884744 | tf_op jit(solution)/shard_map/ppermute | solution.py:242
  18.3 38.0 %collective-permute-start.2 = (f32[2,4,24,384]{3,2,1,0:T(8,128)S(1)}, f32[2,4,24,384]{3,2,1,0:T(8,128)S(1)}, u32[]{:S(2)}, u32[]{:S(2)}) collective-permute-start(f32[2,4,24,384]{3,2,1,0:T(8,128)S(1)} %get-tuple-element.18), channel_id=1, source_target_pairs={{0,4},{1,5},{2,6},{3,7},{4,0},{5,1},{6,2},{7,3},{8,12},{9,13},{10,... | collective-permute-start | bytes 884744 | tf_op jit(solution)/shard_map/ppermute | solution.py:242
  20.2 5.2 %copy-start.3 = (f32[1,256]{1,0:T(1,128)S(1)}, f32[1,256]{1,0:T(1,128)}, u32[]{:S(2)}) copy-start(f32[1,256]{1,0:T(1,128)} %param.5) | copy-start | bytes 3076
  20.2 36.1 %collective-permute-start.3 = (f32[2,4,24,384]{3,2,1,0:T(8,128)S(1)}, f32[2,4,24,384]{3,2,1,0:T(8,128)S(1)}, u32[]{:S(2)}, u32[]{:S(2)}) collective-permute-start(f32[2,4,24,384]{3,2,1,0:T(8,128)S(1)} %get-tuple-element.19), channel_id=1, source_target_pairs={{0,6},{1,7},{2,0},{3,1},{4,2},{5,3},{6,4},{7,5},{8,14},{9,15},{10,... | collective-permute-start | bytes 884744 | tf_op jit(solution)/shard_map/ppermute | solution.py:242
  57.1 15.2 %all-to-all-start.1 = ((f32[8,24,384]{2,1,0:T(8,128)}), f32[8,24,384]{2,1,0:T(8,128)S(1)}, u32[]{:S(2)}, u32[]{:S(2)}) async-start(f32[8,24,384]{2,1,0:T(8,128)} %shard_map.59), calls=%async_computation.1 | async-start | bytes 589824 | tf_op jit(solution)/shard_map/all_to_all | solution.py:256
  62.9 0.7 copy-start.4

commit v3 on v2

--- a/solution.py
+++ b/solution.py
@@ -10,6 +10,7 @@
 MARGIN = 64
 VMEM = pl.BlockSpec(memory_space=pltpu.VMEM)
 SMEM = pl.BlockSpec(memory_space=pltpu.SMEM)
+ANY = pl.BlockSpec(memory_space=pl.ANY)
 
 
 def call(kernel, outs, in_specs, scratch=(), flops=0, moved=0):
@@ -80,11 +81,12 @@
     return out_re, out_im
 
 
-def read_taps(tap_ref, count):
-    return [(tap_ref[k], tap_ref[count + k]) for k in range(count)]
-
-
-def pack_kernel(quarters, where_ref, adj_ref, src_ref, got_ref, *refs):
+def read_taps(tap_ref, slot, count):
+    first = slot * 2 * count
+    return [(tap_ref[first + k], tap_ref[first + count + k]) for k in range(count)]
+
+
+def pack_kernel(quarters, where_ref, adj_ref, src_ref, got_ref, _, *refs):
     outs, pad_ref = refs[:-1], refs[-1]
     core, quarter = where_ref[0], where_ref[1]
     cells = adj_ref.shape[-1]
@@ -112,7 +114,7 @@
 def forward_kernel(quarters, count, where_ref, tap_ref, *refs):
     ins, (adj_ref, mid_ref), pad_ref = refs[:quarters], refs[quarters : quarters + 2], refs[-1]
     quarter = where_ref[1]
-    taps = read_taps(tap_ref, count)
+    taps = read_taps(tap_ref, where_ref[0], count)
     lines, span = ins[0].shape[-2], ins[0].shape[-1]
     for part in range(2):
         pad_ref[part, :8] = jnp.zeros((8, span), jnp.float32)
@@ -154,11 +156,11 @@
 
 
 def chain_kernel(
-    quarters, cells, count, where_ref, omega_ref, tap_ref, slow_ref, adj_ref, mid_ref, out_ref, mu_ref, pad_ref
+    quarters, cells, freqs, count, where_ref, index_ref, tap_ref, slow_ref, adj_ref, mid_ref, out_ref, mu_ref, pad_ref
 ):
     quarter = where_ref[1]
-    omega = omega_ref[0]
-    taps = read_taps(tap_ref, count)
+    omega = 8.0 * (index_ref[where_ref[0]].astype(jnp.float32) + 1.0) / freqs
+    taps = read_taps(tap_ref, where_ref[0], count)
     steps, lines, span = slow_ref.shape
     width = cells // quarters
     for part in range(2):
@@ -217,25 +219,24 @@
     depth = lax.axis_index("depth")
     core, quarter = depth % CORES, depth // CORES
     where = jnp.stack([core, quarter]).astype(jnp.int32)
-    chosen = lax.dynamic_index_in_dim(freq_index, core, 0, False)
-    tap_row = lax.dynamic_index_in_dim(taps, chosen, 0, False).reshape(-1)
-    omega = (8.0 * (chosen.astype(jnp.float32) + 1.0) / count).reshape(1)
+    onehot = freq_index[:, None] == jnp.arange(count, dtype=jnp.int32)[None, :]
+    tap_rows = jnp.sum(jnp.where(onehot[:, :, None, None], taps[None], 0.0), axis=1).reshape(-1)
 
     adj, src = adjoint_source[:, 0], source_top[:, 0]
-    other = jnp.where(core == 0, jnp.stack([adj[1], src[1]]), jnp.stack([adj[0], src[0]]))
+    other = jnp.stack([lax.dynamic_index_in_dim(a, 1 - core, 0, False) for a in (adj, src)])
     got = lax.ppermute(other, "depth", [(d, d ^ 1) for d in range(sections)])
 
-    spread = jnp.broadcast_to(slowness, (groups, block))
-    plane = lax.all_to_all(spread, "freq", 0, 0, tiled=True)
+    spread = jnp.broadcast_to(slowness[None], (groups, 1, block))
+    plane = lax.all_to_all(spread, "freq", 0, 0, tiled=True).reshape(groups, block)
 
     windows = call(
         functools.partial(pack_kernel, quarters),
         [(2, 4, lines, span)] * quarters,
-        [SMEM, VMEM, VMEM, VMEM],
+        [SMEM, VMEM, VMEM, VMEM, ANY],
         [pltpu.VMEM((2, 4, lines, cells + 256), jnp.float32)],
         flops=1 << 20,
         moved=4 << 20,
-    )(where, adj, src, got)
+    )(where, adj, src, got, spread)
     arrived = [windows[0]]
     for k in range(1, quarters):
         hop = [(d, (d + CORES * k) % sections) for d in range(sections)]
@@ -262,10 +263,10 @@
         [pltpu.VMEM((2, lines + 16, span), jnp.float32)],
         flops=1 << 24,
         moved=4 << 20,
-    )(where, tap_row, *arrived)
+    )(where, tap_rows, *arrived)
 
     image = call(
-        functools.partial(chain_kernel, quarters, cells, points),
+        functools.partial(chain_kernel, quarters, cells, count, points),
         [(sections, lines, width)],
         [SMEM, SMEM, SMEM, VMEM, VMEM, VMEM],
         [
@@ -274,7 +275,7 @@
         ],
         flops=1 << 25,
         moved=4 << 20,
-    )(where, omega, tap_row, slow, adj_all, mid_all)
+    )(where, freq_index, tap_rows, slow, adj_all, mid_all)
 
     image = lax.all_to_all(image, "depth", 0, 0, tiled=True)
     rows = call(

time: 109 us -> 109 us (level)
  waiting for transfers between devices: 3.27 us -> 7.03 us
  between operations: 2.75 us -> 0.16 us
  local copies, waits for them, and re-layouts: 2.97 us -> 1.41 us
    all_to_all x1, waiting for transfers between devices: 2.03 us -> 5.79 us  [on_device(): slow = lax.all_to_all(slow, 'depth', 0, 0, tiled=True)]
    slice x1 -> x0, local copies, waits for them, and re-layouts: 1.28 us -> none  [on_device(): src[0]]
  transfers between devices with their start and end apart: 5 -> 5, of which waited for: 2 -> 2; matrix products, arithmetic and copies ran while one was open for 1% -> 0% of each run, Pallas kernels for 3% -> 3%
where the time goes in v3:
time: 109 us; the launch traced here: 108 us
  blocking collectives  61.9 us (57%)
  starting transfers between devices  27.5 us (25%)
  Pallas kernels  8.72 us (8%)
  waiting for transfers between devices  7.03 us (6%)
  local copies, waits for them, and re-layouts  1.41 us (1%)
    all_to_all x1, blocking collectives, on_device(): lax.all_to_all(spread, 'freq', 0, 0, tiled=True).reshape(groups, block)  30.8 us
    all_to_all x1, blocking collectives, on_device(): rows = lax.all_to_all(rows, 'freq', 0, 0, tiled=True)  21.1 us
    ppermute x1, starting transfers between devices, on_device(): got = lax.ppermute(other, 'depth', [(d, d ^ 1) for d in range(sections)])  12.6 us
    all_to_all x1, blocking collectives, on_device(): image = lax.all_to_all(image, 'depth', 0, 0, tiled=True)  9.93 us
    ppermute x3, starting transfers between devices, on_device(): arrived.append(lax.ppermute(windows[k], 'depth', hop))  9 us
    all_to_all x1, starting transfers between devices, on_device(): slow = lax.all_to_all(slow, 'depth', 0, 0, tiled=True)  5.93 us
    all_to_all x1, waiting for transfers between devices, on_device(): slow = lax.all_to_all(slow, 'depth', 0, 0, tiled=True)  5.79 us
    pallas_call x1, Pallas kernels, on_device(): call(functools.partial(chain_kernel, quarters, cells, count, points), [(s...  3.56 us
  transfers between devices with their start and end apart: 5, of which 2 were waited for; matrix products, arithmetic and copies ran while one was open for 0% of the time, Pallas kernels for 3%

profile of v3, /device:TPU:1, one launch (start us, length us, event | category | flops | bytes accessed | tf_op | source)
XLA Modules:
  0.0 107.6 jit_solution(17071985185308360824)
XLA Ops:
  0.0 1.0 dynamic-slice_bitcast_fusion
  1.1 0.0 copy-start
  1.1 0.0 copy-start.1
  1.1 12.6 %collective-permute-start = (f32[2,2,24,1024]{3,2,1,0:T(8,128)S(1)}, f32[2,2,24,1024]{3,2,1,0:T(8,128)S(1)}, u32[]{:S(2)}, u32[]{:S(2)}) collective-permute-start(f32[2,2,24,1024]{3,2,1,0:T(8,128)S(1)} %pad_maximum_fusion), channel_id=1, source_target_pairs={{0,1},{1,0},{2,3},{3,2},{4,5},{5,4},{6,7},{7,6},{8,9},{9,8},{10,11... | collective-permute-start | bytes 1179656 | tf_op jit(solution)/shard_map/ppermute | solution.py:227
  13.7 0.1 pad_add_fusion.where_ref
  13.8 0.0 copy-start.4
  13.8 1.2 %collective-permute-done.got_ref = f32[2,2,24,1024]{3,2,1,0:T(8,128)S(1)} collective-permute-done((f32[2,2,24,1024]{3,2,1,0:T(8,128)S(1)}, f32[2,2,24,1024]{3,2,1,0:T(8,128)S(1)}, u32[]{:S(2)}, u32[]{:S(2)}) %collective-permute-start) | collective-permute-done | bytes 393248 | tf_op jit(solution)/shard_map/ppermute | solution.py:227
  15.0 0.0 copy-done.4
  15.0 0.1 broadcast_in_dim.37._
  15.1 0.0 copy-done
  15.1 0.0 copy-done.1
  15.1 1.1 shard_map.55
  16.2 1.9 %collective-permute-start.1 = (f32[2,4,24,384]{3,2,1,0:T(8,128)S(1)}, f32[2,4,24,384]{3,2,1,0:T(8,128)S(1)}, u32[]{:S(2)}, u32[]{:S(2)}) collective-permute-start(f32[2,4,24,384]{3,2,1,0:T(8,128)S(1)} %get-tuple-element.17), channel_id=1, source_target_pairs={{0,2},{1,3},{2,4},{3,5},{4,6},{5,7},{6,0},{7,1},{8,10},{9,11},{10,... | collective-permute-start | bytes 884744 | tf_op jit(solution)/shard_map/ppermute | solution.py:243
  18.1 1.9 %collective-permute-start.2 = (f32[2,4,24,384]{3,2,1,0:T(8,128)S(1)}, f32[2,4,24,384]{3,2,1,0:T(8,128)S(1)}, u32[]{:S(2)}, u32[]{:S(2)}) collective-permute-start(f32[2,4,24,384]{3,2,1,0:T(8,128)S(1)} %get-tuple-element.18), channel_id=1, source_target_pairs={{0,4},{1,5},{2,6},{3,7},{4,0},{5,1},{6,2},{7,3},{8,12},{9,13},{10,... | collective-permute-start | bytes 884744 | tf_op jit(solution)/shard_map/ppermute | solution.py:243
  20.0 5.2 %collective-permute-start.3 = (f32[2,4,24,384]{3,2,1,0:T(8,128)S(1)}, f32[2,4,24,384]{3,2,1,0:T(8,128)S(1)}, u32[]{:S(2)}, u32[]{:S(2)}) collective-permute-start(f32[2,4,24,384]{3,2,1,0:T(8,128)S(1)} %get-tuple-element.19), channel_id=1, source_target_pairs={{0,6},{1,7},{2,0},{3,1},{4,2},{5,3},{6,4},{7,5},{8,14},{9,15},{10,... | collective-permute-start | bytes 884744 | tf_op jit(solution)/shard_map/ppermute | solution.py:243
  25.2 30.8 %all_to_all.24 = f32[96,1,256]{2,1,0:T(1,128)S(1)} all-to-all(f32[96,1,256]{2,1,0:T(1,128)S(1)} %broadcast_in_dim.37._), channel_id=1, replica_groups=mesh['freq'=96,'depth'=8] {'freq'}, dimensions={0} | all-to-all | bytes 196608 | tf_op jit(solution)/shard_map/all_to_all | solution.py:230
  56.0 0.0 collective-permute-done.1.refs_1_
  56.0 0.0 collective-permute-done.2.refs_2_
  56.0 0.0 collective-permute-done.3.refs_3_
  56.0 0.8 shard_map.56
  56.9 0.0 copy-start.2
  56.9 0.0 copy-start.3
  56.9 5.9 %all-to-all-start.1 = ((f32[8,24,384]{2,1,0:T(8,128)}), f32[8,24,384]{2,1,0:T(8,128)S(1)}, u32[]{:S(2)}, u32[]{:S(2)}) async-start(f32[8,24,384]{2,1,0:T(8,128)} %shard_map.56), calls=%async_computation.1 | async-start | bytes 589824 | tf_op jit(solution)/shard_map/all_to_all | solution.py:257
  62.8 0.0 copy-done.2
  62.8 0.1 iota_compare_fusion
  62.9 0.0 copy-done.3
  62.9 0.1 select_reduce_fusion
  63.0 0.1 copy.10
  63.1 0.1 reshape.45.tap_ref
  63.2 3.2 %shard_map.57 = (f32[8,2,24,384]{3,2,1,0:T(8,128)S(1)}, f32[8,2,24,384]{3,2,1,0:T(8,128)S(1)}) custom-call(s32[2]{0:T(128)S(1)} %pad_add_fusion.where_ref, f32[44]{0:T(128)S(1)} %reshape.45.tap_ref, f32[2,4,24,384]{3,2,1,0:T(8,128)S(1)} %get-tuple-element.21.refs_0_, f32[2,4,24,384]{3,2,1,0:T(8,128)S(1)} %collective-permute-done.1.refs_1_, ...), custom_call_target="tpu_custom_call" | custom-call | flops 16777216 | bytes 4194304 | tf_op jit(solution)/shard_map/pallas_call | solution.py:259
  66.4 5.8 %all-to-all-done.1.slow_ref = f32[8,24,384]{2,1,0:T(8,128)S(1)} async-done(((f32[8,24,384]{2,1,0:T(8,128)}), f32[8,24,384]{2,1,0:T(8,128)S(1)}, u32[]{:S(2)}, u32[]{:S(2)}) %all-to-all-start.1) | async-done | bytes 294944 | tf_op jit(solution)/shard_map/all_to_all | solution.py:257
  72.2 3.6 %shard_map.58 = f32[8,24,256]{2,1,0:T(8,128)S(1)} custom-call(s32[2]{0:T(128)S(1)} %pad_add_fusion.where_ref, s32[2]{0:T(128)S(1)} %copy-done.2, f32[44]{0:T(128)S(1)} %reshape.45.tap_ref, f32[8,24,384]{2,1,0:T(8,128)S(1)} %all-to-all-done.1.slow_ref, f32[8,2,24,384]{3,2,1,0:T(8,128)S(1)} %get-tuple-element.25.adj_ref, ...), custom_call_target="tpu_custom_call" | custom-call | flops 33554432 | bytes 4194304 | tf_op jit(solution)/shard_map/pallas_call | solution.py:268
  75.8 9.9 %all_to_all.25.in_ref = f32[8,24,256]{2,1,0:T(8,128)S(1)} all-to-all(f32[8,24,256]{2,1,0:T(8,128)S(1)} %shard_map.58), channel_id=1, replica_groups=mesh['freq'=96,'depth'=8] {'depth'}, dimensions={0} | all-to-all | bytes 393216 | tf_op jit(solution)/shard_map/all_to_all | solution.py:280
  85.7 0.1 copy.11
  85.8 21.1 %all_to_all.26 = f32[96,1,256]{2,1,0:T(1,128)S(1)} all-to-all(f32[96,1,256]{2,1,0:T(1,128)S(1)} %copy.11), channel_id=1, replica_groups=mesh['freq'=96,'depth'=8] {'freq'}, dimensions={0} | all-to-all | bytes 196608 | tf_op jit(solution)/shard_map/all_to_all | solution.py:289
  107.0 0.1 reduce_sum.19
  107.1 0.6 broadcast_multiply_fusion
  (3 shorter events, 0.1 us)
Async XLA Ops:
  1.1 14.0 %copy-start = (f32[2,1,2,24,1024]{4,3,2,1,0:T(8,128)S(1)}, f32[2,1,2,24,1024]{4,3,2,1,0:T(8,128)}, u32[]{:S(2)}) copy-start(f32[2,1,2,24,1024]{4,3,2,1,0:T(8,128)} %param.9) | copy-start | bytes 1179652
  1.1 14.0 %copy-start.1 = (f32[2,1,2,24,1024]{4,3,2,1,0:T(8,128)S(1)}, f32[2,1,2,24,1024]{4,3,2,1,0:T(8,128)}, u32[]{:S(2)}) copy-start(f32[2,1,2,24,1024]{4,3,2,1,0:T(8,128)} %param.8) | copy-start | bytes 1179652
  1.1 13.9 %collective-permute-start = (f32[2,2,24,1024]{3,2,1,0:T(8,128)S(1)}, f32[2,2,24,1024]{3,2,1,0:T(8,128)S(1)}, u32[]{:S(2)}, u32[]{:S(2)}) collective-permute-start(f32[2,2,24,1024]{3,2,1,0:T(8,128)S(1)} %pad_maximum_fusion), channel_id=1, source_target_pairs={{0,1},{1,0},{2,3},{3,2},{4,5},{5,4},{6,7},{7,6},{8,9},{9,8},{10,11... | collective-permute-start | bytes 1179656 | tf_op jit(solution)/shard_map/ppermute | solution.py:227
  13.8 1.2 %copy-start.4 = (f32[1,256]{1,0:T(1,128)S(1)}, f32[1,256]{1,0:T(1,128)}, u32[]{:S(2)}) copy-start(f32[1,256]{1,0:T(1,128)} %param.5) | copy-start | bytes 3076
  16.2 39.8 %collective-permute-start.1 = (f32[2,4,24,384]{3,2,1,0:T(8,128)S(1)}, f32[2,4,24,384]{3,2,1,0:T(8,128)S(1)}, u32[]{:S(2)}, u32[]{:S(2)}) collective-permute-start(f32[2,4,24,384]{3,2,1,0:T(8,128)S(1)} %get-tuple-element.17), channel_id=1, source_target_pairs={{0,2},{1,3},{2,4},{3,5},{4,6},{5,7},{6,0},{7,1},{8,10},{9,11},{10,... | collective-permute-start | bytes 884744 | tf_op jit(solution)/shard_map/ppermute | solution.py:243
  18.1 37.9 %collective-permute-start.2 = (f32[2,4,24,384]{3,2,1,0:T(8,128)S(1)}, f32[2,4,24,384]{3,2,1,0:T(8,128)S(1)}, u32[]{:S(2)}, u32[]{:S(2)}) collective-permute-start(f32[2,4,24,384]{3,2,1,0:T(8,128)S(1)} %get-tuple-element.18), channel_id=1, source_target_pairs={{0,4},{1,5},{2,6},{3,7},{4,0},{5,1},{6,2},{7,3},{8,12},{9,13},{10,... | collective-permute-start | bytes 884744 | tf_op jit(solution)/shard_map/ppermute | solution.py:243
  20.0 36.0 %collective-permute-start.3 = (f32[2,4,24,384]{3,2,1,0:T(8,128)S(1)}, f32[2,4,24,384]{3,2,1,0:T(8,128)S(1)}, u32[]{:S(2)}, u32[]{:S(2)}) collective-permute-start(f32[2,4,24,384]{3,2,1,0:T(8,128)S(1)} %get-tuple-element.19), channel_id=1, source_target_pairs={{0,6},{1,7},{2,0},{3,1},{4,2},{5,3},{6,4},{7,5},{8,14},{9,15},{10,... | collective-permute-start | bytes 884744 | tf_op jit(solution)/shard_map/ppermute | solution.py:243
  56.9 5.9 %copy-start.2 = (s32[2]{0:T(128)S(1)}, s32[2]{0:T(128)}, u32[]{:S(2)}) copy-start(s32[2]{0:T(128)} %index_ref.1) | copy-start | bytes 28
  56.9 6.0 %copy-start.3 = (f32[192,2,11]{0,1,2:T(2,128)S(1)}, f32[192,2,11]{0,1,2:T(2,128)}, u32[]{:S(2)}) copy-start(f32[192,2,11]{0,1,2:T(2,128)} %param.7) | copy-start | bytes 50692
  56.9 15.3 %all-to-all-start.1 = ((f32[8,24,384]{2,1,0:T(8,128)}), f32[8,24,384]{2,1,0:T(8,128)S(1)}, u32[]{:S(2)}, u32[]{:S(2)}) async-start(f32[8,24,384]{2,1,0:T(8,128)} %shard_map.56), calls=%async_computation.1 | async-start | bytes 589824 | tf_op jit(solution)/shard_map/all_to_all | solution.py:257

commit v4 on v3

--- a/solution.py
+++ b/solution.py
@@ -237,10 +237,10 @@
         flops=1 << 20,
         moved=4 << 20,
     )(where, adj, src, got, spread)
-    arrived = [windows[0]]
-    for k in range(1, quarters):
+    arrived = [windows[0]] * quarters
+    for k in sorted(range(1, quarters), key=lambda k: -min(k, quarters - k)):
         hop = [(d, (d + CORES * k) % sections) for d in range(sections)]
-        arrived.append(lax.ppermute(windows[k], "depth", hop))
+        arrived[k] = lax.ppermute(windows[k], "depth", hop)
 
     plane, *arrived = lax.optimization_barrier((plane, *arrived))
     slow = call(

time: 109 us -> 109 us (level)
  no operation moved by 1% of the time
where the time goes in v4:
time: 109 us; the launch traced here: 108 us
  blocking collectives  61.9 us (57%)
  starting transfers between devices  27.5 us (25%)
  Pallas kernels  8.72 us (8%)
  waiting for transfers between devices  7.03 us (6%)
  local copies, waits for them, and re-layouts  1.41 us (1%)
    all_to_all x1, blocking collectives, on_device(): lax.all_to_all(spread, 'freq', 0, 0, tiled=True).reshape(groups, block)  30.8 us
    all_to_all x1, blocking collectives, on_device(): rows = lax.all_to_all(rows, 'freq', 0, 0, tiled=True)  21.1 us
    ppermute x1, starting transfers between devices, on_device(): got = lax.ppermute(other, 'depth', [(d, d ^ 1) for d in range(sections)])  12.6 us
    all_to_all x1, blocking collectives, on_device(): image = lax.all_to_all(image, 'depth', 0, 0, tiled=True)  9.93 us
    ppermute x3, starting transfers between devices, on_device(): arrived[k] = lax.ppermute(windows[k], 'depth', hop)  9 us
    all_to_all x1, starting transfers between devices, on_device(): slow = lax.all_to_all(slow, 'depth', 0, 0, tiled=True)  5.93 us
    all_to_all x1, waiting for transfers between devices, on_device(): slow = lax.all_to_all(slow, 'depth', 0, 0, tiled=True)  5.79 us
    pallas_call x1, Pallas kernels, on_device(): call(functools.partial(chain_kernel, quarters, cells, count, points), [(s...  3.56 us
  transfers between devices with their start and end apart: 5, of which 2 were waited for; matrix products, arithmetic and copies ran while one was open for 0% of the time, Pallas kernels for 3%

profile of v4, /device:TPU:1, one launch (start us, length us, event | category | flops | bytes accessed | tf_op | source)
XLA Modules:
  0.0 107.6 jit_solution(17071985185308360824)
XLA Ops:
  0.0 1.0 dynamic-slice_bitcast_fusion
  1.1 0.0 copy-start
  1.1 0.0 copy-start.1
  1.1 12.6 %collective-permute-start = (f32[2,2,24,1024]{3,2,1,0:T(8,128)S(1)}, f32[2,2,24,1024]{3,2,1,0:T(8,128)S(1)}, u32[]{:S(2)}, u32[]{:S(2)}) collective-permute-start(f32[2,2,24,1024]{3,2,1,0:T(8,128)S(1)} %pad_maximum_fusion), channel_id=1, source_target_pairs={{0,1},{1,0},{2,3},{3,2},{4,5},{5,4},{6,7},{7,6},{8,9},{9,8},{10,11... | collective-permute-start | bytes 1179656 | tf_op jit(solution)/shard_map/ppermute | solution.py:227
  13.7 0.1 pad_add_fusion.where_ref
  13.8 0.0 copy-start.4
  13.8 1.2 %collective-permute-done.got_ref = f32[2,2,24,1024]{3,2,1,0:T(8,128)S(1)} collective-permute-done((f32[2,2,24,1024]{3,2,1,0:T(8,128)S(1)}, f32[2,2,24,1024]{3,2,1,0:T(8,128)S(1)}, u32[]{:S(2)}, u32[]{:S(2)}) %collective-permute-start) | collective-permute-done | bytes 393248 | tf_op jit(solution)/shard_map/ppermute | solution.py:227
  15.0 0.0 copy-done.4
  15.0 0.1 broadcast_in_dim.37._
  15.1 0.0 copy-done
  15.1 0.0 copy-done.1
  15.1 1.1 shard_map.55
  16.2 1.9 %collective-permute-start.1 = (f32[2,4,24,384]{3,2,1,0:T(8,128)S(1)}, f32[2,4,24,384]{3,2,1,0:T(8,128)S(1)}, u32[]{:S(2)}, u32[]{:S(2)}) collective-permute-start(f32[2,4,24,384]{3,2,1,0:T(8,128)S(1)} %get-tuple-element.17), channel_id=1, source_target_pairs={{0,2},{1,3},{2,4},{3,5},{4,6},{5,7},{6,0},{7,1},{8,10},{9,11},{10,... | collective-permute-start | bytes 884744 | tf_op jit(solution)/shard_map/ppermute | solution.py:243
  18.1 1.9 %collective-permute-start.2 = (f32[2,4,24,384]{3,2,1,0:T(8,128)S(1)}, f32[2,4,24,384]{3,2,1,0:T(8,128)S(1)}, u32[]{:S(2)}, u32[]{:S(2)}) collective-permute-start(f32[2,4,24,384]{3,2,1,0:T(8,128)S(1)} %get-tuple-element.18), channel_id=1, source_target_pairs={{0,4},{1,5},{2,6},{3,7},{4,0},{5,1},{6,2},{7,3},{8,12},{9,13},{10,... | collective-permute-start | bytes 884744 | tf_op jit(solution)/shard_map/ppermute | solution.py:243
  20.0 5.2 %collective-permute-start.3 = (f32[2,4,24,384]{3,2,1,0:T(8,128)S(1)}, f32[2,4,24,384]{3,2,1,0:T(8,128)S(1)}, u32[]{:S(2)}, u32[]{:S(2)}) collective-permute-start(f32[2,4,24,384]{3,2,1,0:T(8,128)S(1)} %get-tuple-element.19), channel_id=1, source_target_pairs={{0,6},{1,7},{2,0},{3,1},{4,2},{5,3},{6,4},{7,5},{8,14},{9,15},{10,... | collective-permute-start | bytes 884744 | tf_op jit(solution)/shard_map/ppermute | solution.py:243
  25.2 30.8 %all_to_all.24 = f32[96,1,256]{2,1,0:T(1,128)S(1)} all-to-all(f32[96,1,256]{2,1,0:T(1,128)S(1)} %broadcast_in_dim.37._), channel_id=1, replica_groups=mesh['freq'=96,'depth'=8] {'freq'}, dimensions={0} | all-to-all | bytes 196608 | tf_op jit(solution)/shard_map/all_to_all | solution.py:230
  56.0 0.0 collective-permute-done.1.refs_1_
  56.0 0.0 collective-permute-done.2.refs_2_
  56.0 0.0 collective-permute-done.3.refs_3_
  56.0 0.8 shard_map.56
  56.9 0.0 copy-start.2
  56.9 0.0 copy-start.3
  56.9 5.9 %all-to-all-start.1 = ((f32[8,24,384]{2,1,0:T(8,128)}), f32[8,24,384]{2,1,0:T(8,128)S(1)}, u32[]{:S(2)}, u32[]{:S(2)}) async-start(f32[8,24,384]{2,1,0:T(8,128)} %shard_map.56), calls=%async_computation.1 | async-start | bytes 589824 | tf_op jit(solution)/shard_map/all_to_all | solution.py:257
  62.8 0.0 copy-done.2
  62.8 0.1 iota_compare_fusion
  62.9 0.0 copy-done.3
  62.9 0.1 select_reduce_fusion
  63.0 0.1 copy.10
  63.1 0.1 reshape.45.tap_ref
  63.2 3.2 %shard_map.57 = (f32[8,2,24,384]{3,2,1,0:T(8,128)S(1)}, f32[8,2,24,384]{3,2,1,0:T(8,128)S(1)}) custom-call(s32[2]{0:T(128)S(1)} %pad_add_fusion.where_ref, f32[44]{0:T(128)S(1)} %reshape.45.tap_ref, f32[2,4,24,384]{3,2,1,0:T(8,128)S(1)} %get-tuple-element.21.refs_0_, f32[2,4,24,384]{3,2,1,0:T(8,128)S(1)} %collective-permute-done.1.refs_1_, ...), custom_call_target="tpu_custom_call" | custom-call | flops 16777216 | bytes 4194304 | tf_op jit(solution)/shard_map/pallas_call | solution.py:259
  66.4 5.8 %all-to-all-done.1.slow_ref = f32[8,24,384]{2,1,0:T(8,128)S(1)} async-done(((f32[8,24,384]{2,1,0:T(8,128)}), f32[8,24,384]{2,1,0:T(8,128)S(1)}, u32[]{:S(2)}, u32[]{:S(2)}) %all-to-all-start.1) | async-done | bytes 294944 | tf_op jit(solution)/shard_map/all_to_all | solution.py:257
  72.2 3.6 %shard_map.58 = f32[8,24,256]{2,1,0:T(8,128)S(1)} custom-call(s32[2]{0:T(128)S(1)} %pad_add_fusion.where_ref, s32[2]{0:T(128)S(1)} %copy-done.2, f32[44]{0:T(128)S(1)} %reshape.45.tap_ref, f32[8,24,384]{2,1,0:T(8,128)S(1)} %all-to-all-done.1.slow_ref, f32[8,2,24,384]{3,2,1,0:T(8,128)S(1)} %get-tuple-element.25.adj_ref, ...), custom_call_target="tpu_custom_call" | custom-call | flops 33554432 | bytes 4194304 | tf_op jit(solution)/shard_map/pallas_call | solution.py:268
  75.8 9.9 %all_to_all.25.in_ref = f32[8,24,256]{2,1,0:T(8,128)S(1)} all-to-all(f32[8,24,256]{2,1,0:T(8,128)S(1)} %shard_map.58), channel_id=1, replica_groups=mesh['freq'=96,'depth'=8] {'depth'}, dimensions={0} | all-to-all | bytes 393216 | tf_op jit(solution)/shard_map/all_to_all | solution.py:280
  85.7 0.1 copy.11
  85.8 21.1 %all_to_all.26 = f32[96,1,256]{2,1,0:T(1,128)S(1)} all-to-all(f32[96,1,256]{2,1,0:T(1,128)S(1)} %copy.11), channel_id=1, replica_groups=mesh['freq'=96,'depth'=8] {'freq'}, dimensions={0} | all-to-all | bytes 196608 | tf_op jit(solution)/shard_map/all_to_all | solution.py:289
  107.0 0.1 reduce_sum.19
  107.1 0.6 broadcast_multiply_fusion
  (3 shorter events, 0.1 us)
Async XLA Ops:
  1.1 14.0 %copy-start = (f32[2,1,2,24,1024]{4,3,2,1,0:T(8,128)S(1)}, f32[2,1,2,24,1024]{4,3,2,1,0:T(8,128)}, u32[]{:S(2)}) copy-start(f32[2,1,2,24,1024]{4,3,2,1,0:T(8,128)} %param.9) | copy-start | bytes 1179652
  1.1 14.0 %copy-start.1 = (f32[2,1,2,24,1024]{4,3,2,1,0:T(8,128)S(1)}, f32[2,1,2,24,1024]{4,3,2,1,0:T(8,128)}, u32[]{:S(2)}) copy-start(f32[2,1,2,24,1024]{4,3,2,1,0:T(8,128)} %param.8) | copy-start | bytes 1179652
  1.1 13.9 %collective-permute-start = (f32[2,2,24,1024]{3,2,1,0:T(8,128)S(1)}, f32[2,2,24,1024]{3,2,1,0:T(8,128)S(1)}, u32[]{:S(2)}, u32[]{:S(2)}) collective-permute-start(f32[2,2,24,1024]{3,2,1,0:T(8,128)S(1)} %pad_maximum_fusion), channel_id=1, source_target_pairs={{0,1},{1,0},{2,3},{3,2},{4,5},{5,4},{6,7},{7,6},{8,9},{9,8},{10,11... | collective-permute-start | bytes 1179656 | tf_op jit(solution)/shard_map/ppermute | solution.py:227
  13.8 1.2 %copy-start.4 = (f32[1,256]{1,0:T(1,128)S(1)}, f32[1,256]{1,0:T(1,128)}, u32[]{:S(2)}) copy-start(f32[1,256]{1,0:T(1,128)} %param.5) | copy-start | bytes 3076
  16.2 39.8 %collective-permute-start.1 = (f32[2,4,24,384]{3,2,1,0:T(8,128)S(1)}, f32[2,4,24,384]{3,2,1,0:T(8,128)S(1)}, u32[]{:S(2)}, u32[]{:S(2)}) collective-permute-start(f32[2,4,24,384]{3,2,1,0:T(8,128)S(1)} %get-tuple-element.17), channel_id=1, source_target_pairs={{0,2},{1,3},{2,4},{3,5},{4,6},{5,7},{6,0},{7,1},{8,10},{9,11},{10,... | collective-permute-start | bytes 884744 | tf_op jit(solution)/shard_map/ppermute | solution.py:243
  18.1 37.9 %collective-permute-start.2 = (f32[2,4,24,384]{3,2,1,0:T(8,128)S(1)}, f32[2,4,24,384]{3,2,1,0:T(8,128)S(1)}, u32[]{:S(2)}, u32[]{:S(2)}) collective-permute-start(f32[2,4,24,384]{3,2,1,0:T(8,128)S(1)} %get-tuple-element.18), channel_id=1, source_target_pairs={{0,4},{1,5},{2,6},{3,7},{4,0},{5,1},{6,2},{7,3},{8,12},{9,13},{10,... | collective-permute-start | bytes 884744 | tf_op jit(solution)/shard_map/ppermute | solution.py:243
  20.0 36.0 %collective-permute-start.3 = (f32[2,4,24,384]{3,2,1,0:T(8,128)S(1)}, f32[2,4,24,384]{3,2,1,0:T(8,128)S(1)}, u32[]{:S(2)}, u32[]{:S(2)}) collective-permute-start(f32[2,4,24,384]{3,2,1,0:T(8,128)S(1)} %get-tuple-element.19), channel_id=1, source_target_pairs={{0,6},{1,7},{2,0},{3,1},{4,2},{5,3},{6,4},{7,5},{8,14},{9,15},{10,... | collective-permute-start | bytes 884744 | tf_op jit(solution)/shard_map/ppermute | solution.py:243
  56.9 5.9 %copy-start.2 = (s32[2]{0:T(128)S(1)}, s32[2]{0:T(128)}, u32[]{:S(2)}) copy-start(s32[2]{0:T(128)} %index_ref.1) | copy-start | bytes 28
  56.9 6.0 %copy-start.3 = (f32[192,2,11]{0,1,2:T(2,128)S(1)}, f32[192,2,11]{0,1,2:T(2,128)}, u32[]{:S(2)}) copy-start(f32[192,2,11]{0,1,2:T(2,128)} %param.7) | copy-start | bytes 50692
  56.9 15.3 %all-to-all-start.1 = ((f32[8,24,384]{2,1,0:T(8,128)}), f32[8,24,384]{2,1,0:T(8,128)S(1)}, u32[]{:S(2)}, u32[]{:S(2)}) async-start(f32[8,24,384]{2,1,0:T(8,128)} %shard_map.56), calls=%async_computation.1 | async-start | bytes 589824 | tf_op jit(solution)/shard_map/all_to_all | solution.py:257
